TPU v7x, 256 devices: a whole 4x4x8 slice. The times are simulated.
256 devices in a mesh: wide: 32 (over z, y), slab: 8 (over x, core).
Axes of the slice: x: 4, y: 4, z: 8, core: 2. Of those that a mesh axis runs over, the one named last changes fastest.
Arguments:
- thermal_state: float32 [32, 128, 32, 1024], P('wide', 'slab'), may hold values from -5 to 5
- thermal_spreading_rate: bfloat16 [32, 128, 32, 1024], P('wide', 'slab'), may hold values from 0.5 to 1.5
- flow_speed_vector: bfloat16 [3, 32, 128, 32, 1024], P(None, 'wide', 'slab'), may hold values from -0.796875 to 0.796875
- interface_guess: float32 [32, 2048], P('wide', 'slab'), may hold values from -4 to 4
- partner_facing_rows: int32 [32, 2048], P('wide', 'slab'), may hold values from 0 to 2047, each once within a row
- mismatch_change_matrix: float32 [32, 2048, 128], P('wide', 'slab'), may hold values from -5 to 5
- output_change_matrix: float32 [32, 2048, 128], P('wide', 'slab'), may hold values from -1.8 to 1.8
Outputs:
- temperature_out: float32 [32, 128, 32, 1024], P('wide', 'slab')
- updated_interface_guess: float32 [32, 2048], P('wide', 'slab')
- unitary_basis_factor: float32 [32, 2048, 128], P('wide', 'slab')
Inputs may be any that keep to these rules, and one draw needn't show every extreme that they name: `partner_facing_rows`: each partition's rows of matching are a permutation of its partner's interface rows.
All inputs are finite; a program needn't handle non-finite values.
Results may differ from a plain program's by a relative error of at most 0.0003.
Values may be sent and summed in bfloat16 or wider, within the bound.
No kernel may reach another device: no remote copies, remote signals or barrier semaphores. Data moves between devices by JAX's collectives and lax.ppermute only.
A program may use at most 64 MiB of HBM per device.

v0:
```python
import math
import jax
import jax.numpy as jnp
from jax import lax
from jax.sharding import PartitionSpec as P

INTERFACE_STRIP = 64
SWEEPS = 4
STEP_SIZE = 0.11


def padded(cells, sides, width):
    for axis, dim in sides:
        count = lax.axis_size(axis)
        ends = count - 1
        head = lax.slice_in_dim(cells, 0, width, axis=dim)
        tail = lax.slice_in_dim(cells, cells.shape[dim] - width, cells.shape[dim], axis=dim)
        cells = jnp.concatenate(
            [
                lax.ppermute(tail, axis, [(i, (i + 1) % count) for i in range(ends)]),
                cells,
                lax.ppermute(head, axis, [((i + 1) % count, i) for i in range(ends)]),
            ],
            axis=dim,
        )
    return cells


def partner(value, axis, stride):
    mask = 2**stride
    pairs = [(source, source ^ mask) for source in range(lax.axis_size(axis))]
    return lax.ppermute(value, axis, pairs)


def surround_wrapper(block_rows, mirror_layer):
    bottom = jnp.zeros((block_rows.shape[0], 1, block_rows.shape[2]), block_rows.dtype)
    stacked = jnp.concatenate([bottom, block_rows, mirror_layer[:, None, :]], axis=1)
    return jnp.pad(stacked, ((0, 0), (0, 0), (1, 1)))


def march_forward(bordered_array, diffuse_subdomain, subdomain_flow_speed):
    centre = bordered_array[1:-1, 1:-1, 1:-1]
    plus_first = bordered_array[2:, 1:-1, 1:-1]
    minus_first = bordered_array[:-2, 1:-1, 1:-1]
    plus_second = bordered_array[1:-1, 2:, 1:-1]
    minus_second = bordered_array[1:-1, :-2, 1:-1]
    plus_third = bordered_array[1:-1, 1:-1, 2:]
    minus_third = bordered_array[1:-1, 1:-1, :-2]
    spread = (
        plus_first
        + minus_first
        + plus_second
        + minus_second
        + plus_third
        + minus_third
        - 6.0 * centre
    )
    carried = 0.5 * (
        subdomain_flow_speed[0].astype(jnp.float32) * (plus_first - minus_first)
        + subdomain_flow_speed[1].astype(jnp.float32) * (plus_second - minus_second)
        + subdomain_flow_speed[2].astype(jnp.float32) * (plus_third - minus_third)
    )
    return centre + STEP_SIZE * (diffuse_subdomain.astype(jnp.float32) * spread - carried)


def shards(
    thermal_state,
    thermal_spreading_rate,
    flow_speed_vector,
    interface_guess,
    partner_facing_rows,
    mismatch_change_matrix,
    output_change_matrix,
):
    subdomain_thermal_state = thermal_state[0]
    diffuse_subdomain = thermal_spreading_rate[0]
    subdomain_flow_speed = flow_speed_vector[:, 0]
    layer_stack = subdomain_thermal_state.shape[0]
    vertical_extent = subdomain_thermal_state.shape[1]
    rows_dev = interface_guess.shape[1]
    mirror_layer = jnp.repeat(interface_guess[0].reshape(layer_stack, -1), INTERFACE_STRIP, axis=1)
    panel = mismatch_change_matrix[0]
    gram_local = lax.dot_general(
        panel,
        panel,
        (((0,), (0,)), ((), ())),
        precision=lax.Precision.HIGHEST,
        preferred_element_type=jnp.float32,
    )
    ghost_padded = jnp.pad(mirror_layer, ((1, 1), (0, 0)))
    for sweep in range(SWEEPS):
        widened_array = padded(subdomain_thermal_state, (("slab", 0),), 1)
        subdomain_thermal_state = march_forward(
            surround_wrapper(widened_array, ghost_padded), diffuse_subdomain, subdomain_flow_speed
        )
    face_means = jnp.mean(
        subdomain_thermal_state[:, vertical_extent - 1, :].reshape(
            layer_stack, -1, INTERFACE_STRIP
        ),
        axis=2,
    )
    face_means = face_means.reshape(1, rows_dev)
    top_bit = lax.axis_size("wide").bit_length() - 2
    partner_own = partner(face_means, "wide", top_bit)
    partner_all = lax.all_gather(partner_own, "slab", axis=1, tiled=True)
    tilde = jnp.take(partner_all[0], partner_facing_rows[0], axis=0)
    resid = tilde - interface_guess[0]
    proj_local = jnp.dot(
        resid, panel, precision=lax.Precision.HIGHEST, preferred_element_type=jnp.float32
    )
    gram_matrix, projection = lax.psum((gram_local, proj_local), ("wide", "slab"))
    lower_factor = jnp.linalg.cholesky(gram_matrix)
    half_solve = lax.linalg.triangular_solve(
        lower_factor, projection[:, None], left_side=True, lower=True
    )
    coefficients = -lax.linalg.triangular_solve(
        lower_factor, half_solve, left_side=True, lower=True, transpose_a=True
    )[:, 0]
    update = jnp.dot(
        output_change_matrix[0],
        coefficients,
        precision=lax.Precision.HIGHEST,
        preferred_element_type=jnp.float32,
    )
    updated_interface_guess = tilde + update
    total_rows = rows_dev * lax.axis_size("slab") * lax.axis_size("wide")
    scaled = lax.linalg.triangular_solve(
        lower_factor, panel, left_side=False, lower=True, transpose_a=True
    )
    unitary_basis_factor = math.sqrt(total_rows) * scaled
    return (
        subdomain_thermal_state[None],
        updated_interface_guess[None],
        unitary_basis_factor[None],
    )


def solution(mesh):
    return jax.shard_map(
        shards,
        mesh=mesh,
        in_specs=(
            P("wide", "slab", None, None),
            P("wide", "slab", None, None),
            P(None, "wide", "slab", None, None),
            P("wide", "slab"),
            P("wide", "slab"),
            P("wide", "slab", None),
            P("wide", "slab", None),
        ),
        out_specs=(P("wide", "slab", None, None), P("wide", "slab"), P("wide", "slab", None)),
        check_vma=False,
    )
```

profile of v0, /device:TPU:1, one launch (start us, length us, event | category | flops | bytes accessed | tf_op | source)
XLA Modules:
  0.0 438.8 jit_solution(339822084845978649)
XLA Ops:
  7.2 0.0 copy-start
  7.2 0.0 all-reduce.11.cloned.1.call-start
  7.2 1.0 slice_bitcast_fusion
  8.2 5.1 %collective-permute-start = (f32[1,32,1024]{2,1,0:T(8,128)S(1)}, f32[1,32,1024]{2,1,0:T(8,128)S(1)}, u32[]{:S(2)}, u32[]{:S(2)}) collective-permute-start(f32[1,32,1024]{2,1,0:T(8,128)S(1)} %get-tuple-element.16), channel_id=1, source_target_pairs={{1,0},{2,1},{3,2},{4,3},{5,4},{6,5},{7,6},{9,8},{10,9},{11,10},{12... | collective-permute-start | bytes 393224 | tf_op jit(solution)/shard_map/ppermute | solution.py:22
  13.4 1.9 collective-permute-start.1
  15.3 1.0 fusion.39
  16.4 0.0 all-reduce.11.cloned.1.call-update
  16.4 0.7 compare_select_fusion.1
  17.1 0.5 broadcast.243
  17.6 1.3 reduce.11
  18.9 0.1 reshape_squeeze.6
  19.0 0.1 broadcast_in_dim.29
  19.1 0.1 reshape.95
  19.2 0.1 broadcast_in_dim.30
  19.3 237.0 %all-reduce.11.cloned.1.call-done = f32[128,128]{0,1:T(8,128)} async-done(((f32[128,128]{0,1:T(8,128)}), f32[128,128]{0,1:T(8,128)}) %all-reduce.11.cloned.1.call-update) | async-done | bytes 65552 | tf_op jit(solution)/shard_map/psum | solution.py:111
  256.3 0.9 copy.14
  257.2 0.0 copy-start.10
  257.3 0.6 copy-done.10
  257.9 2.3 pad_maximum_fusion.3
  260.2 0.3 copy-done.1
  260.5 0.3 copy-done.6
  260.7 7.0 %fusion.2 = f32[16,32,1024]{2,1,0:T(8,128)S(1)} fusion(f32[16,32,1024]{2,1,0:T(8,128)} %bitcast.90, f32[18,34,1024]{2,1,0:T(8,128)S(1)} %pad_maximum_fusion.3, f32[1,32,1024]{2,1,0:T(8,128)S(1)} %collective-permute-done, f32[1,32,1024]{2,1,0:T(8,128)S(1)} %copy-done.11, f32[18,1,1024]{2,1,0:T(1,128)S(1)} %broadcast_in_dim.30, ...), kind=kLoop, calls=%fused_computation.35 | loop fusion | flops 18874368 | bytes 11231232 | tf_op jit(solution)/shard_map/add | solution.py:63
  267.8 1.3 copy-done.4
  269.1 0.7 fusion.61
  269.8 1.9 collective-permute-start.2
  271.7 3.6 collective-permute-start.3
  275.4 0.6 fusion.45
  276.0 12.5 %cholesky.16 = f32[128,128]{1,0:T(8,128)S(1)} custom-call(f32[128,128]{1,0:T(8,128)} %fusion.45), custom_call_target="Cholesky" | custom-call | tf_op jit(solution)/shard_map/jit(cholesky)/cholesky | solution.py:112
  288.6 0.0 copy-start.5
  288.6 2.3 pad_maximum_fusion.2
  290.9 0.2 copy-done.7
  291.1 4.6 %fusion.5 = f32[16,32,1024]{2,1,0:T(8,128)S(1)} fusion(f32[16,32,1024]{2,1,0:T(8,128)S(1)} %copy-done.5, f32[18,34,1024]{2,1,0:T(8,128)S(1)} %pad_maximum_fusion.2, f32[1,32,1024]{2,1,0:T(8,128)S(1)} %collective-permute-done.2, f32[1,32,1024]{2,1,0:T(8,128)} %collective-permute-done.3, f32[18,1,1024]{2,1,0:T(1,128)S(1)} %broadcast_in_dim.30, ...), kind=kLoop, calls=%fused_computation.38 | loop fusion | flops 18874368 | bytes 11231232 | tf_op jit(solution)/shard_map/add | solution.py:63
  295.8 1.9 collective-permute-start.4
  297.7 3.8 collective-permute-start.5
  301.6 0.6 compare_reduce_fusion
  302.2 1.1 collective-permute-done.5
  303.3 0.7 pad_maximum_fusion.1
  304.0 5.4 %fusion.8 = f32[16,32,1024]{2,1,0:T(8,128)S(1)} fusion(f32[16,32,1024]{2,1,0:T(8,128)S(1)} %fusion.5, f32[18,34,1024]{2,1,0:T(8,128)S(1)} %pad_maximum_fusion.1, f32[1,32,1024]{2,1,0:T(8,128)S(1)} %collective-permute-done.4, f32[1,32,1024]{2,1,0:T(8,128)S(1)} %collective-permute-done.5, f32[18,1,1024]{2,1,0:T(1,128)S(1)} %broadcast_in_dim.30, ...), kind=kLoop, calls=%fused_computation.41 | loop fusion | flops 18874368 | bytes 11231232 | tf_op jit(solution)/shard_map/add | solution.py:63
  309.4 1.3 copy-done.2
  310.7 0.7 fusion.59
  311.4 1.9 collective-permute-start.6
  313.3 4.4 collective-permute-start.7
  317.7 1.3 fusion.41
  319.0 10.6 %custom-call.10 = f32[1,128,128]{1,2,0:T(8,128)S(1)} custom-call(f32[1,128,128]{2,1,0:T(8,128)} %fusion.41), custom_call_target="InvertDiagBlocksLowerTriangular" | custom-call | tf_op jit(solution)/shard_map/triangular_solve | solution.py:116
  329.7 2.3 pad_maximum_fusion
  332.0 0.2 copy-done.8
  332.2 4.6 %fusion.11 = f32[16,32,1024]{2,1,0:T(8,128)S(1)} fusion(f32[16,32,1024]{2,1,0:T(8,128)S(1)} %copy-done.3, f32[18,34,1024]{2,1,0:T(8,128)S(1)} %pad_maximum_fusion, f32[1,32,1024]{2,1,0:T(8,128)S(1)} %collective-permute-done.6, f32[1,32,1024]{2,1,0:T(8,128)} %collective-permute-done.7, f32[18,1,1024]{2,1,0:T(1,128)S(1)} %broadcast_in_dim.30, ...), kind=kLoop, calls=%fused_computation.44 | loop fusion | flops 18874368 | bytes 11231232 | tf_op jit(solution)/shard_map/add | solution.py:63
  336.8 1.3 copy-done.9
  338.2 0.2 slice_reduce_fusion
  338.3 0.1 reshape_squeeze.7
  338.4 0.1 reduce_sum.9
  338.5 0.1 div.18
  338.6 0.9 collective-permute-start.8
  339.5 0.3 fusion.32
  339.8 0.8 copy.15
  340.6 4.4 %collective-permute-done.8 = f32[1,256]{1,0:T(1,128)S(1)} collective-permute-done((f32[1,256]{1,0:T(1,128)S(1)}, f32[1,256]{1,0:T(1,128)S(1)}, u32[]{:S(2)}, u32[]{:S(2)}) %collective-permute-start.8) | collective-permute-done | bytes 1056 | tf_op jit(solution)/shard_map/ppermute | solution.py:32
  345.0 10.1 %all_gather.3 = f32[1,2048]{1,0:T(1,128)S(1)} all-gather(f32[1,256]{1,0:T(1,128)S(1)} %collective-permute-done.8), channel_id=1, replica_groups=mesh['wide'=32,'slab'=8] {'slab'}, dimensions={1}, use_global_device_ids=true | all-gather | bytes 9216 | tf_op jit(solution)/shard_map/all_gather | solution.py:105
  355.1 1.7 gather_fusion
  356.8 0.2 convolution_bitcast_fusion.2
  357.0 73.7 %psum.15 = f32[128]{0:T(128)S(1)} all-reduce(f32[128]{0:T(128)S(1)} %convolution_bitcast_fusion.2), channel_id=1, replica_groups=mesh['wide'=32,'slab'=8] {'wide','slab'}, use_global_device_ids=true, to_apply=%region_4.5 | all-reduce | flops 128 | bytes 1024 | tf_op jit(solution)/shard_map/psum | solution.py:111
  430.7 0.2 convolution_bitcast_fusion.1
  430.9 0.2 fusion.34
  431.1 0.2 fusion.35
  431.3 0.6 fusion.46
  (38 shorter events, 0.2 us)
Async XLA Ops:
  7.2 8.2 %copy-start = (f32[1,256,128]{2,1,0:T(8,128)S(1)}, f32[1,256,128]{2,1,0:T(8,128)}, u32[]{:S(2)}) copy-start(f32[1,256,128]{2,1,0:T(8,128)} %param.12) | copy-start | bytes 393220
  7.2 249.1 %all-reduce.11.cloned.1.call-start = ((), (), s32[]{:S(2)}) async-start(), calls=%async_computation | async-start | bytes 131072 | tf_op jit(solution)/shard_map/psum | solution.py:111
  8.2 249.0 %collective-permute-start = (f32[1,32,1024]{2,1,0:T(8,128)S(1)}, f32[1,32,1024]{2,1,0:T(8,128)S(1)}, u32[]{:S(2)}, u32[]{:S(2)}) collective-permute-start(f32[1,32,1024]{2,1,0:T(8,128)S(1)} %get-tuple-element.16), channel_id=1, source_target_pairs={{1,0},{2,1},{3,2},{4,3},{5,4},{6,5},{7,6},{9,8},{10,9},{11,10},{12... | collective-permute-start | bytes 393224 | tf_op jit(solution)/shard_map/ppermute | solution.py:22
  13.4 243.8 %collective-permute-start.1 = (f32[1,32,1024]{2,1,0:T(8,128)S(1)}, f32[1,32,1024]{2,1,0:T(8,128)S(1)}, u32[]{:S(2)}, u32[]{:S(2)}) collective-permute-start(f32[1,32,1024]{2,1,0:T(8,128)S(1)} %get-tuple-element.15), channel_id=1, source_target_pairs={{0,1},{1,2},{2,3},{3,4},{4,5},{5,6},{6,7},{8,9},{9,10},{10,11},{11... | collective-permute-start | bytes 393224 | tf_op jit(solution)/shard_map/ppermute | solution.py:20
  257.2 0.7 copy-start.10
  257.9 2.6 copy-start.1
  257.9 2.8 copy-start.6
  257.9 2.8 copy-start.11
  260.7 14.6 %copy-start.12 = (f32[128,128]{0,1:T(8,128)S(1)}, f32[128,128]{0,1:T(8,128)}, u32[]{:S(2)}) copy-start(f32[128,128]{0,1:T(8,128)} %all-reduce.11.cloned.1.call-done) | copy-start | bytes 196612
  267.8 1.3 copy-start.4
  269.8 18.8 %collective-permute-start.2 = (f32[1,32,1024]{2,1,0:T(8,128)}, f32[1,32,1024]{2,1,0:T(8,128)S(1)}, u32[]{:S(2)}, u32[]{:S(2)}) collective-permute-start(f32[1,32,1024]{2,1,0:T(8,128)} %get-tuple-element.14), channel_id=1, source_target_pairs={{1,0},{2,1},{3,2},{4,3},{5,4},{6,5},{7,6},{9,8},{10,9},{11,10},{12... | collective-permute-start | bytes 393224 | tf_op jit(solution)/shard_map/ppermute | solution.py:22
  271.7 16.9 %collective-permute-start.3 = (f32[1,32,1024]{2,1,0:T(8,128)}, f32[1,32,1024]{2,1,0:T(8,128)}, u32[]{:S(2)}, u32[]{:S(2)}) collective-permute-start(f32[1,32,1024]{2,1,0:T(8,128)} %get-tuple-element.13), channel_id=1, source_target_pairs={{0,1},{1,2},{2,3},{3,4},{4,5},{5,6},{6,7},{8,9},{9,10},{10,11},{11... | collective-permute-start | bytes 393224 | tf_op jit(solution)/shard_map/ppermute | solution.py:20
  288.6 13.0 %copy-start.13 = (f32[128,128]{1,0:T(8,128)}, f32[128,128]{1,0:T(8,128)S(1)}, u32[]{:S(2)}) copy-start(f32[128,128]{1,0:T(8,128)S(1)} %cholesky.16) | copy-start | bytes 196612
  288.6 2.3 copy-start.5
  288.6 2.5 copy-start.7
  295.8 6.4 %collective-permute-start.4 = (f32[1,32,1024]{2,1,0:T(8,128)S(1)}, f32[1,32,1024]{2,1,0:T(8,128)S(1)}, u32[]{:S(2)}, u32[]{:S(2)}) collective-permute-start(f32[1,32,1024]{2,1,0:T(8,128)S(1)} %get-tuple-element.12), channel_id=1, source_target_pairs={{1,0},{2,1},{3,2},{4,3},{5,4},{6,5},{7,6},{9,8},{10,9},{11,10},{12... | collective-permute-start | bytes 393224 | tf_op jit(solution)/shard_map/ppermute | solution.py:22
  297.7 5.6 %collective-permute-start.5 = (f32[1,32,1024]{2,1,0:T(8,128)S(1)}, f32[1,32,1024]{2,1,0:T(8,128)S(1)}, u32[]{:S(2)}, u32[]{:S(2)}) collective-permute-start(f32[1,32,1024]{2,1,0:T(8,128)S(1)} %get-tuple-element.11), channel_id=1, source_target_pairs={{0,1},{1,2},{2,3},{3,4},{4,5},{5,6},{6,7},{8,9},{9,10},{10,11},{11... | collective-permute-start | bytes 393224 | tf_op jit(solution)/shard_map/ppermute | solution.py:20
  304.0 13.7 %copy-start.14 = (f32[128,128]{1,0:T(8,128)S(1)}, f32[128,128]{1,0:T(8,128)}, u32[]{:S(2)}) copy-start(f32[128,128]{1,0:T(8,128)} %copy-done.13) | copy-start | bytes 196612
  309.4 1.3 copy-start.2
  311.4 18.2 %collective-permute-start.6 = (f32[1,32,1024]{2,1,0:T(8,128)}, f32[1,32,1024]{2,1,0:T(8,128)S(1)}, u32[]{:S(2)}, u32[]{:S(2)}) collective-permute-start(f32[1,32,1024]{2,1,0:T(8,128)} %get-tuple-element.10), channel_id=1, source_target_pairs={{1,0},{2,1},{3,2},{4,3},{5,4},{6,5},{7,6},{9,8},{10,9},{11,10},{12... | collective-permute-start | bytes 393224 | tf_op jit(solution)/shard_map/ppermute | solution.py:22
  313.3 16.3 %collective-permute-start.7 = (f32[1,32,1024]{2,1,0:T(8,128)}, f32[1,32,1024]{2,1,0:T(8,128)}, u32[]{:S(2)}, u32[]{:S(2)}) collective-permute-start(f32[1,32,1024]{2,1,0:T(8,128)} %get-tuple-element.9), channel_id=1, source_target_pairs={{0,1},{1,2},{2,3},{3,4},{4,5},{5,6},{6,7},{8,9},{9,10},{10,11},{11... | collective-permute-start | bytes 393224 | tf_op jit(solution)/shard_map/ppermute | solution.py:20
  329.6 2.3 copy-start.3
  329.7 2.5 copy-start.8
  336.8 1.3 copy-start.9
  338.2 18.6 %copy-start.16 = (s32[1,256]{1,0:T(1,128)S(1)}, s32[1,256]{1,0:T(1,128)}, u32[]{:S(2)}) copy-start(s32[1,256]{1,0:T(1,128)} %param.11) | copy-start | bytes 3076
  338.2 18.6 %copy-start.17 = (f32[1,256]{1,0:T(1,128)S(1)}, f32[1,256]{1,0:T(1,128)}, u32[]{:S(2)}) copy-start(f32[1,256]{1,0:T(1,128)} %param.10) | copy-start | bytes 3076
  338.2 92.9 %copy-start.15 = (f32[1,256,128]{2,1,0:T(8,128)S(1)}, f32[1,256,128]{2,1,0:T(8,128)}, u32[]{:S(2)}) copy-start(f32[1,256,128]{2,1,0:T(8,128)} %param.13) | copy-start | bytes 393220
  338.6 6.4 %collective-permute-start.8 = (f32[1,256]{1,0:T(1,128)S(1)}, f32[1,256]{1,0:T(1,128)S(1)}, u32[]{:S(2)}, u32[]{:S(2)}) collective-permute-start(f32[1,256]{1,0:T(1,128)S(1)} %div.18), channel_id=1, source_target_pairs={{0,128},{8,136},{16,144},{24,152},{32,160},{40,168},{48,176},{56,1... | collective-permute-start | bytes 3080 | tf_op jit(solution)/shard_map/ppermute | solution.py:32
Sparse Core Ops, SparseCore 0:
  16.5 239.7 all-reduce.10
where the time goes:
time: 439 us
  waiting for transfers between devices  242 us (55%)
  blocking collectives  83.8 us (19%)
  other arithmetic  57.7 us (13%)
  starting transfers between devices  25.5 us (6%)
  between operations  14.5 us (3%)
  local copies, waits for them, and re-layouts  12.7 us (3%)
    psum x1, waiting for transfers between devices, shards(): lax.psum((gram_local, proj_local), ('wide', 'slab'))  237 us
    psum x1, blocking collectives, shards(): lax.psum((gram_local, proj_local), ('wide', 'slab'))  73.7 us
    add x4, other arithmetic, march_forward(): centre + STEP_SIZE * (diffuse_subdomain.astype(jnp.float32) * spread - ca...  21.7 us
    ppermute x4, starting transfers between devices, padded(): lax.ppermute(tail, axis, [(i, (i + 1) % count) for i in range(ends)])  13.7 us
    another operation x3, other arithmetic, shards(): lower_factor = jnp.linalg.cholesky(gram_matrix)  13.2 us
    another operation x2, other arithmetic, shards(): lax.linalg.triangular_solve(lower_factor, half_solve, left_side=True, low...  11.9 us
    ppermute x4, starting transfers between devices, padded(): lax.ppermute(head, axis, [((i + 1) % count, i) for i in range(ends)])  10.9 us
    all_gather x1, blocking collectives, shards(): partner_all = lax.all_gather(partner_own, 'slab', axis=1, tiled=True)  10.1 us
  transfers between devices with their start and end apart: 10, of which 3 were waited for; matrix products, arithmetic and copies ran while one was open for 7% of the time, Pallas kernels for 0%

commit v1 on v0

--- a/solution.py
+++ b/solution.py
@@ -108,7 +108,9 @@
     proj_local = jnp.dot(
         resid, panel, precision=lax.Precision.HIGHEST, preferred_element_type=jnp.float32
     )
-    gram_matrix, projection = lax.psum((gram_local, proj_local), ("wide", "slab"))
+    gram_matrix, projection = lax.psum(
+        lax.psum((gram_local, proj_local), axis_name="slab"), axis_name="wide"
+    )
     lower_factor = jnp.linalg.cholesky(gram_matrix)
     half_solve = lax.linalg.triangular_solve(
         lower_factor, projection[:, None], left_side=True, lower=True

time: 439 us -> 416 us (0.948)
  the two profiles are of different devices: /device:TPU:1 before, /device:TPU:0 now
where the time goes in v1:
time: 416 us; the launch traced here: 415 us
  waiting for transfers between devices  209 us (50%)
  blocking collectives  97.5 us (23%)
  other arithmetic  56.3 us (14%)
  starting transfers between devices  23.4 us (6%)
  between operations  14.4 us (3%)
  local copies, waits for them, and re-layouts  12.7 us (3%)
    psum x1, waiting for transfers between devices, shards(): lax.psum(lax.psum((gram_local, proj_local), axis_name='slab'), axis_name=...  142 us
    psum x1, blocking collectives, shards(): lax.psum(lax.psum((gram_local, proj_local), axis_name='slab'), axis_name=...  72.9 us
    psum x1, waiting for transfers between devices, shards(): lax.psum((gram_local, proj_local), axis_name='slab')  62.9 us
    add x4, other arithmetic, march_forward(): centre + STEP_SIZE * (diffuse_subdomain.astype(jnp.float32) * spread - ca...  21.7 us
    ppermute x4, starting transfers between devices, padded(): lax.ppermute(tail, axis, [(i, (i + 1) % count) for i in range(ends)])  15.8 us
    another operation x3, other arithmetic, shards(): lower_factor = jnp.linalg.cholesky(gram_matrix)  13.2 us
    psum x1, blocking collectives, shards(): lax.psum((gram_local, proj_local), axis_name='slab')  12.7 us
    all_gather x1, blocking collectives, shards(): partner_all = lax.all_gather(partner_own, 'slab', axis=1, tiled=True)  11.8 us
  transfers between devices with their start and end apart: 11, of which 4 were waited for; matrix products, arithmetic and copies ran while one was open for 7% of the time, Pallas kernels for 0%

profile of v1, /device:TPU:0, one launch (start us, length us, event | category | flops | bytes accessed | tf_op | source)
XLA Modules:
  0.0 415.4 jit_solution(10058338562083767768)
XLA Ops:
  7.2 0.0 all-reduce.12.cloned.1.call-start
  7.2 1.0 slice_bitcast_fusion
  8.2 1.3 collective-permute-start
  9.5 3.0 collective-permute-start.1
  12.6 1.0 fusion.39
  13.6 0.0 all-reduce.12.cloned.1.call-update
  13.6 0.0 all-reduce.14.cloned.1.call-start
  13.7 0.7 compare_select_fusion.1
  14.4 0.5 broadcast.243
  14.9 1.3 reduce.11
  16.2 0.1 reshape_squeeze.6
  16.3 0.1 broadcast_in_dim.29
  16.4 0.1 reshape.95
  16.5 0.1 broadcast_in_dim.30
  16.6 62.9 %all-reduce.12.cloned.1.call-done = f32[128,128]{0,1:T(8,128)} async-done(((f32[128,128]{0,1:T(8,128)}), f32[128,128]{0,1:T(8,128)}) %all-reduce.12.cloned.1.call-update) | async-done | bytes 65552 | tf_op jit(solution)/shard_map/psum | solution.py:112
  79.6 141.9 %all-reduce.14.cloned.1.call-done = f32[128,128]{0,1:T(8,128)} async-done(((f32[128,128]{0,1:T(8,128)}), f32[128,128]{0,1:T(8,128)}) %all-reduce.14.cloned.1.call-update) | async-done | bytes 65552 | tf_op jit(solution)/shard_map/psum | solution.py:111
  221.5 0.9 copy.14
  222.4 0.6 copy-done.10
  223.1 2.3 pad_maximum_fusion.3
  225.3 0.3 copy-done.1
  225.6 0.3 copy-done.6
  225.9 7.0 %fusion.2 = f32[16,32,1024]{2,1,0:T(8,128)S(1)} fusion(f32[16,32,1024]{2,1,0:T(8,128)} %bitcast.90, f32[18,34,1024]{2,1,0:T(8,128)S(1)} %pad_maximum_fusion.3, f32[1,32,1024]{2,1,0:T(8,128)S(1)} %collective-permute-done, f32[1,32,1024]{2,1,0:T(8,128)S(1)} %copy-done.11, f32[18,1,1024]{2,1,0:T(1,128)S(1)} %broadcast_in_dim.30, ...), kind=kLoop, calls=%fused_computation.35 | loop fusion | flops 18874368 | bytes 11231232 | tf_op jit(solution)/shard_map/add | solution.py:63
  232.9 1.3 copy-done.4
  234.2 0.7 fusion.61
  235.0 1.3 collective-permute-start.2
  236.2 3.7 collective-permute-start.3
  239.9 0.6 fusion.45
  240.6 12.5 %cholesky.16 = f32[128,128]{1,0:T(8,128)S(1)} custom-call(f32[128,128]{1,0:T(8,128)} %fusion.45), custom_call_target="Cholesky" | custom-call | tf_op jit(solution)/shard_map/jit(cholesky)/cholesky | solution.py:114
  253.2 2.3 pad_maximum_fusion.2
  255.5 0.2 copy-done.7
  255.7 4.6 %fusion.5 = f32[16,32,1024]{2,1,0:T(8,128)S(1)} fusion(f32[16,32,1024]{2,1,0:T(8,128)S(1)} %copy-done.5, f32[18,34,1024]{2,1,0:T(8,128)S(1)} %pad_maximum_fusion.2, f32[1,32,1024]{2,1,0:T(8,128)S(1)} %collective-permute-done.2, f32[1,32,1024]{2,1,0:T(8,128)} %collective-permute-done.3, f32[18,1,1024]{2,1,0:T(1,128)S(1)} %broadcast_in_dim.30, ...), kind=kLoop, calls=%fused_computation.38 | loop fusion | flops 18874368 | bytes 11231232 | tf_op jit(solution)/shard_map/add | solution.py:63
  260.3 1.3 collective-permute-start.4
  261.6 3.2 collective-permute-start.5
  264.9 0.6 compare_reduce_fusion
  265.5 0.1 collective-permute-done.5
  265.6 0.7 pad_maximum_fusion.1
  266.3 5.4 %fusion.8 = f32[16,32,1024]{2,1,0:T(8,128)S(1)} fusion(f32[16,32,1024]{2,1,0:T(8,128)S(1)} %fusion.5, f32[18,34,1024]{2,1,0:T(8,128)S(1)} %pad_maximum_fusion.1, f32[1,32,1024]{2,1,0:T(8,128)S(1)} %collective-permute-done.4, f32[1,32,1024]{2,1,0:T(8,128)S(1)} %collective-permute-done.5, f32[18,1,1024]{2,1,0:T(1,128)S(1)} %broadcast_in_dim.30, ...), kind=kLoop, calls=%fused_computation.41 | loop fusion | flops 18874368 | bytes 11231232 | tf_op jit(solution)/shard_map/add | solution.py:63
  271.7 1.3 copy-done.2
  273.1 0.7 fusion.59
  273.8 1.3 collective-permute-start.6
  275.1 5.8 %collective-permute-start.7 = (f32[1,32,1024]{2,1,0:T(8,128)}, f32[1,32,1024]{2,1,0:T(8,128)}, u32[]{:S(2)}, u32[]{:S(2)}) collective-permute-start(f32[1,32,1024]{2,1,0:T(8,128)} %get-tuple-element.9), channel_id=1, source_target_pairs={{0,1},{1,2},{2,3},{3,4},{4,5},{5,6},{6,7},{8,9},{9,10},{10,11},{11... | collective-permute-start | bytes 393224 | tf_op jit(solution)/shard_map/ppermute | solution.py:20
  280.9 0.7 fusion.41
  281.5 9.8 %custom-call.10 = f32[1,128,128]{1,2,0:T(8,128)S(1)} custom-call(f32[1,128,128]{2,1,0:T(8,128)S(1)} %fusion.41), custom_call_target="InvertDiagBlocksLowerTriangular" | custom-call | tf_op jit(solution)/shard_map/triangular_solve | solution.py:118
  291.4 2.3 pad_maximum_fusion
  293.7 0.2 copy-done.8
  293.9 4.7 %fusion.11 = f32[16,32,1024]{2,1,0:T(8,128)S(1)} fusion(f32[16,32,1024]{2,1,0:T(8,128)S(1)} %copy-done.3, f32[18,34,1024]{2,1,0:T(8,128)S(1)} %pad_maximum_fusion, f32[1,32,1024]{2,1,0:T(8,128)} %collective-permute-done.6, f32[1,32,1024]{2,1,0:T(8,128)} %collective-permute-done.7, f32[18,1,1024]{2,1,0:T(1,128)S(1)} %broadcast_in_dim.30, ...), kind=kLoop, calls=%fused_computation.44 | loop fusion | flops 18874368 | bytes 11231232 | tf_op jit(solution)/shard_map/add | solution.py:63
  298.6 1.3 copy-done.9
  300.0 0.2 slice_reduce_fusion
  300.1 0.1 reshape_squeeze.7
  300.2 0.1 reduce_sum.9
  300.4 0.1 div.18
  300.4 2.4 collective-permute-start.8
  302.8 0.3 fusion.32
  303.1 0.8 copy.15
  303.9 4.0 collective-permute-done.8
  307.9 11.8 %all_gather.3 = f32[1,2048]{1,0:T(1,128)S(1)} all-gather(f32[1,256]{1,0:T(1,128)S(1)} %collective-permute-done.8), channel_id=1, replica_groups=mesh['wide'=32,'slab'=8] {'slab'}, dimensions={1}, use_global_device_ids=true | all-gather | bytes 9216 | tf_op jit(solution)/shard_map/all_gather | solution.py:105
  319.8 1.7 gather_fusion
  321.5 0.2 convolution_bitcast_fusion.2
  321.7 12.7 %psum.30 = f32[128]{0:T(128)S(1)} all-reduce(f32[128]{0:T(128)S(1)} %convolution_bitcast_fusion.2), channel_id=1, replica_groups=mesh['wide'=32,'slab'=8] {'slab'}, use_global_device_ids=true, to_apply=%region_5.6 | all-reduce | flops 128 | bytes 1024 | tf_op jit(solution)/shard_map/psum | solution.py:112
  334.4 72.9 %psum.31 = f32[128]{0:T(128)S(1)} all-reduce(f32[128]{0:T(128)S(1)} %psum.30), channel_id=1, replica_groups=mesh['wide'=32,'slab'=8] {'wide'}, use_global_device_ids=true, to_apply=%region_6.7 | all-reduce | flops 128 | bytes 1024 | tf_op jit(solution)/shard_map/psum | solution.py:111
  407.4 0.2 convolution_bitcast_fusion.1
  407.5 0.2 fusion.34
  407.7 0.2 fusion.35
  407.9 0.6 fusion.46
  (38 shorter events, 0.2 us)
Async XLA Ops:
  7.2 5.4 %copy-start = (f32[1,256,128]{2,1,0:T(8,128)S(1)}, f32[1,256,128]{2,1,0:T(8,128)}, u32[]{:S(2)}) copy-start(f32[1,256,128]{2,1,0:T(8,128)} %param.12) | copy-start | bytes 393220
  7.2 72.3 %all-reduce.12.cloned.1.call-start = ((), (), s32[]{:S(2)}) async-start(), calls=%async_computation | async-start | bytes 131072 | tf_op jit(solution)/shard_map/psum | solution.py:112
  8.2 214.1 %collective-permute-start = (f32[1,32,1024]{2,1,0:T(8,128)S(1)}, f32[1,32,1024]{2,1,0:T(8,128)S(1)}, u32[]{:S(2)}, u32[]{:S(2)}) collective-permute-start(f32[1,32,1024]{2,1,0:T(8,128)S(1)} %get-tuple-element.16), channel_id=1, source_target_pairs={{1,0},{2,1},{3,2},{4,3},{5,4},{6,5},{7,6},{9,8},{10,9},{11,10},{12... | collective-permute-start | bytes 393224 | tf_op jit(solution)/shard_map/ppermute | solution.py:22
  9.5 212.9 %collective-permute-start.1 = (f32[1,32,1024]{2,1,0:T(8,128)S(1)}, f32[1,32,1024]{2,1,0:T(8,128)S(1)}, u32[]{:S(2)}, u32[]{:S(2)}) collective-permute-start(f32[1,32,1024]{2,1,0:T(8,128)S(1)} %get-tuple-element.15), channel_id=1, source_target_pairs={{0,1},{1,2},{2,3},{3,4},{4,5},{5,6},{6,7},{8,9},{9,10},{10,11},{11... | collective-permute-start | bytes 393224 | tf_op jit(solution)/shard_map/ppermute | solution.py:20
  13.6 207.8 %all-reduce.14.cloned.1.call-start = ((), (), s32[]{:S(2)}) async-start(), calls=%async_computation.1 | async-start | bytes 131072 | tf_op jit(solution)/shard_map/psum | solution.py:111
  222.4 0.7 copy-start.10
  223.1 2.6 copy-start.1
  223.1 2.8 copy-start.6
  223.1 2.8 copy-start.11
  225.9 14.0 %copy-start.12 = (f32[128,128]{0,1:T(8,128)S(1)}, f32[128,128]{0,1:T(8,128)}, u32[]{:S(2)}) copy-start(f32[128,128]{0,1:T(8,128)} %all-reduce.14.cloned.1.call-done) | copy-start | bytes 196612
  232.9 1.3 copy-start.4
  235.0 18.2 %collective-permute-start.2 = (f32[1,32,1024]{2,1,0:T(8,128)}, f32[1,32,1024]{2,1,0:T(8,128)S(1)}, u32[]{:S(2)}, u32[]{:S(2)}) collective-permute-start(f32[1,32,1024]{2,1,0:T(8,128)} %get-tuple-element.14), channel_id=1, source_target_pairs={{1,0},{2,1},{3,2},{4,3},{5,4},{6,5},{7,6},{9,8},{10,9},{11,10},{12... | collective-permute-start | bytes 393224 | tf_op jit(solution)/shard_map/ppermute | solution.py:22
  236.2 16.9 %collective-permute-start.3 = (f32[1,32,1024]{2,1,0:T(8,128)}, f32[1,32,1024]{2,1,0:T(8,128)}, u32[]{:S(2)}, u32[]{:S(2)}) collective-permute-start(f32[1,32,1024]{2,1,0:T(8,128)} %get-tuple-element.13), channel_id=1, source_target_pairs={{0,1},{1,2},{2,3},{3,4},{4,5},{5,6},{6,7},{8,9},{9,10},{10,11},{11... | collective-permute-start | bytes 393224 | tf_op jit(solution)/shard_map/ppermute | solution.py:20
  253.1 2.3 copy-start.5
  253.1 2.5 copy-start.7
  260.3 5.2 %collective-permute-start.4 = (f32[1,32,1024]{2,1,0:T(8,128)S(1)}, f32[1,32,1024]{2,1,0:T(8,128)S(1)}, u32[]{:S(2)}, u32[]{:S(2)}) collective-permute-start(f32[1,32,1024]{2,1,0:T(8,128)S(1)} %get-tuple-element.12), channel_id=1, source_target_pairs={{1,0},{2,1},{3,2},{4,3},{5,4},{6,5},{7,6},{9,8},{10,9},{11,10},{12... | collective-permute-start | bytes 393224 | tf_op jit(solution)/shard_map/ppermute | solution.py:22
  261.6 4.0 collective-permute-start.5
  271.7 1.3 copy-start.2
  273.8 17.6 %collective-permute-start.6 = (f32[1,32,1024]{2,1,0:T(8,128)}, f32[1,32,1024]{2,1,0:T(8,128)}, u32[]{:S(2)}, u32[]{:S(2)}) collective-permute-start(f32[1,32,1024]{2,1,0:T(8,128)} %get-tuple-element.10), channel_id=1, source_target_pairs={{1,0},{2,1},{3,2},{4,3},{5,4},{6,5},{7,6},{9,8},{10,9},{11,10},{12... | collective-permute-start | bytes 393224 | tf_op jit(solution)/shard_map/ppermute | solution.py:22
  275.1 16.3 %collective-permute-start.7 = (f32[1,32,1024]{2,1,0:T(8,128)}, f32[1,32,1024]{2,1,0:T(8,128)}, u32[]{:S(2)}, u32[]{:S(2)}) collective-permute-start(f32[1,32,1024]{2,1,0:T(8,128)} %get-tuple-element.9), channel_id=1, source_target_pairs={{0,1},{1,2},{2,3},{3,4},{4,5},{5,6},{6,7},{8,9},{9,10},{10,11},{11... | collective-permute-start | bytes 393224 | tf_op jit(solution)/shard_map/ppermute | solution.py:20
  291.4 2.4 copy-start.3
  291.4 2.6 copy-start.8
  298.6 1.3 copy-start.9
  300.0 21.5 %copy-start.14 = (s32[1,256]{1,0:T(1,128)S(1)}, s32[1,256]{1,0:T(1,128)}, u32[]{:S(2)}) copy-start(s32[1,256]{1,0:T(1,128)} %param.11) | copy-start | bytes 3076
  300.0 21.6 %copy-start.15 = (f32[1,256]{1,0:T(1,128)S(1)}, f32[1,256]{1,0:T(1,128)}, u32[]{:S(2)}) copy-start(f32[1,256]{1,0:T(1,128)} %param.10) | copy-start | bytes 3076
  300.0 107.7 %copy-start.13 = (f32[1,256,128]{2,1,0:T(8,128)S(1)}, f32[1,256,128]{2,1,0:T(8,128)}, u32[]{:S(2)}) copy-start(f32[1,256,128]{2,1,0:T(8,128)} %param.13) | copy-start | bytes 393220
  300.4 7.5 %collective-permute-start.8 = (f32[1,256]{1,0:T(1,128)S(1)}, f32[1,256]{1,0:T(1,128)S(1)}, u32[]{:S(2)}, u32[]{:S(2)}) collective-permute-start(f32[1,256]{1,0:T(1,128)S(1)} %div.18), channel_id=1, source_target_pairs={{0,128},{8,136},{16,144},{24,152},{32,160},{40,168},{48,176},{56,1... | collective-permute-start | bytes 3080 | tf_op jit(solution)/shard_map/ppermute | solution.py:32
Sparse Core Ops, SparseCore 0:
  13.8 65.7 all-reduce.11
  83.4 138.0 all-reduce.13
